TPU v7x, 256 devices: a whole 4x4x8 slice. The times are simulated.
256 devices in a mesh: batch: 32 (over z, x), tensor: 8 (over y, core).
Axes of the slice: x: 4, y: 4, z: 8, core: 2. Of those that a mesh axis runs over, the one named last changes fastest.
Arguments:
- tokens: bfloat16 [8192, 4096], P(('batch', 'tensor')), may hold values from -6 to 6
- norm_gain: float32 [4096], replicated, may hold values from 0.1 to 1.9
- w_query: bfloat16 [4096, 4096], P(None, 'tensor'), may hold values from -0.09375 to 0.09375
- w_key: bfloat16 [4096, 1024], P(None, 'tensor'), may hold values from -0.25 to 0.25
- w_value: bfloat16 [4096, 1024], P(None, 'tensor'), may hold values from -0.09375 to 0.09375
- w_out: bfloat16 [4096, 4096], P('tensor'), may hold values from -0.25 to 0.25
- prefix_keys: bfloat16 [16384, 1024], P('batch', 'tensor'), may hold values from -6 to 6
- prefix_values: bfloat16 [16384, 1024], P('batch', 'tensor'), may hold values from -6 to 6
- cache_keys: bfloat16 [147456, 1024], P('batch', 'tensor'), may hold values from -160 to 160
- cache_values: bfloat16 [147456, 1024], P('batch', 'tensor'), may hold values from -6 to 6
- cache_lengths: int32 [128], replicated, may hold values from 128 to 2048, as said below
- prefix_used: int32 [128], P('batch'), may hold values from 4096 to 16384
- parents: int32 [128, 64], P('batch'), may hold values from 0 to 62, as said below
- accepted_index: int32 [128, 8], P('batch'), may hold values from 0 to 63, as said below
Outputs:
- mixed_output: bfloat16 [8192, 4096], P(('batch', 'tensor'))
- accepted_keys: bfloat16 [128, 8, 1024], P('batch', None, 'tensor')
- accepted_values: bfloat16 [128, 8, 1024], P('batch', None, 'tensor')
Inputs may be any that keep to these rules, and one draw needn't show every extreme that they name: `cache_lengths`: within each aligned group of 4 requests at most 2 have more than 256 cached tokens; in the first group exactly that many do, and some request has exactly 2048. parents[r, 0] = 0; for i >= 1, parents[r, i] lies between max(0, i - 8) and i - 1. `accepted_index`: each row lists 8 tree positions, each the parent of the next, ending at a position of 32 or more; where the root is reached the row repeats 0 at its front.
All inputs are finite; a program needn't handle non-finite values.
Results may differ from a plain program's by a relative error of at most 0.015.
The roundings to bfloat16 on the way count: a program that leaves them out, or rounds other values in their place, can miss the bound.
Values may be sent and summed in bfloat16 or wider, within the bound.
A program may use at most 192 MiB of HBM per device.

v0:
```python
import jax
import jax.numpy as jnp
from jax import lax
from jax.sharding import PartitionSpec as P

HD = 128
NEG_FILL = -1e30
HIGHEST = lax.Precision.HIGHEST


def rms_normed(tokens, norm_gain):
    values = tokens.astype(jnp.float32)
    factor = lax.rsqrt(jnp.mean(values * values, axis=-1, keepdims=True) + 1e-05)
    return (values * factor * norm_gain).astype(jnp.bfloat16)


def ancestor_table(parents):
    node_count = parents.shape[-1]
    column = jnp.arange(node_count, dtype=jnp.int32)
    linked = (parents[..., None] == column).astype(jnp.float32)
    itself = (column[:, None] == column[None, :]).astype(jnp.float32)
    ancestry = jnp.minimum(linked + itself, 1.0)
    for repeat in range(node_count.bit_length()):
        ancestry = jnp.minimum(
            jnp.einsum("rij,rjk->rik", ancestry, ancestry, precision=HIGHEST), 1.0
        )
    return ancestry


def rotate(values, positions):
    half_width = values.shape[-1] // 2
    frequency = 10000.0 ** (-jnp.arange(half_width, dtype=jnp.float32) / half_width)
    angles = positions.astype(jnp.float32)[:, None] * frequency[None, :]
    cosine = jnp.cos(angles)[:, None, :]
    sine_table = jnp.sin(angles)[:, None, :]
    first_half = values[..., :half_width]
    second_half = values[..., half_width:]
    return jnp.concatenate(
        [
            first_half * cosine - second_half * sine_table,
            second_half * cosine + first_half * sine_table,
        ],
        axis=-1,
    )


def absorb(carry, scores, visible, apply_values):
    running_max, running_sum, running_out = carry
    masked = jnp.where(visible, scores, NEG_FILL)
    new_max = jnp.maximum(running_max, jnp.max(masked, axis=-1))
    weights = jnp.where(visible, jnp.exp(masked - new_max[..., None]), 0.0)
    factor = jnp.exp(running_max - new_max)
    new_sum = running_sum * factor + jnp.sum(weights, axis=-1)
    new_out = running_out * factor[..., None] + apply_values(weights.astype(jnp.bfloat16))
    return (new_max, new_sum, new_out)


def combine(first_part, second_part):
    joint_max = jnp.maximum(first_part[0], second_part[0])
    first_factor = jnp.exp(first_part[0] - joint_max)
    second_factor = jnp.exp(second_part[0] - joint_max)
    joint_sum = first_part[1] * first_factor + second_part[1] * second_factor
    joint_out = first_part[2] * first_factor[..., None] + second_part[2] * second_factor[..., None]
    return (joint_max, joint_sum, joint_out)


def empty_partials(leading, head_size):
    return (
        jnp.full(leading, NEG_FILL, jnp.float32),
        jnp.zeros(leading, jnp.float32),
        jnp.zeros(leading + (head_size,), jnp.float32),
    )


def cache_partials(queries, all_keys, all_values, lower_slot, upper_slot, score_scale):
    capacity = all_keys.shape[0]
    block_size = min(512, capacity)
    kv_local = queries.shape[1]
    head_size = queries.shape[3]

    def one_request(request_items):
        request_query, lower_bound, upper_bound = request_items
        blocks = (upper_bound - lower_bound + block_size - 1) // block_size

        def block_step(block_index, carry):
            block_begin = lower_bound + block_index * block_size
            start = jnp.clip(block_begin, 0, capacity - block_size)
            block_keys = lax.dynamic_slice_in_dim(all_keys, start, block_size, 0).reshape(
                block_size, kv_local, head_size
            )
            block_values = lax.dynamic_slice_in_dim(all_values, start, block_size, 0).reshape(
                block_size, kv_local, head_size
            )
            slot_ids = start + jnp.arange(block_size, dtype=jnp.int32)
            visible = (slot_ids >= block_begin) & (
                slot_ids < jnp.minimum(upper_bound, block_begin + block_size)
            )
            scores = (
                jnp.einsum(
                    "hqd,khd->hqk", request_query, block_keys, preferred_element_type=jnp.float32
                )
                * score_scale
            )
            return absorb(
                carry,
                scores,
                visible[None, None, :],
                lambda rounded: jnp.einsum(
                    "hqk,khd->hqd", rounded, block_values, preferred_element_type=jnp.float32
                ),
            )

        start_carry = empty_partials(request_query.shape[:2], head_size)
        return lax.fori_loop(0, blocks, block_step, start_carry)

    return lax.map(one_request, (queries, lower_slot, upper_slot))


def body(
    tokens,
    norm_gain,
    w_query,
    w_key,
    w_value,
    w_out,
    prefix_keys,
    prefix_values,
    cache_keys,
    cache_values,
    cache_lengths,
    prefix_used,
    parents,
    accepted_index,
):
    req_count, tree_size = parents.shape
    head_size = HD
    query_cols = w_query.shape[1]
    key_cols = w_key.shape[1]
    kv_local = key_cols // head_size
    group_size = query_cols // key_cols
    query_rows = tree_size * group_size
    score_scale = head_size ** (-0.5)
    normed = rms_normed(tokens, norm_gain)
    piece = lax.all_gather(normed, "tensor", axis=0, tiled=True)
    projected = jnp.concatenate(
        [
            jnp.dot(piece, w_query, preferred_element_type=jnp.float32),
            jnp.dot(piece, w_key, preferred_element_type=jnp.float32),
            jnp.dot(piece, w_value, preferred_element_type=jnp.float32),
        ],
        axis=1,
    )
    group_index = lax.axis_index("batch")
    own_lengths = lax.dynamic_slice_in_dim(cache_lengths, group_index * req_count, req_count)
    ancestry = ancestor_table(parents)
    tree_depth = (jnp.sum(ancestry, axis=-1) - 1.0).astype(jnp.int32)
    position = ((prefix_used + own_lengths)[:, None] + tree_depth).reshape(req_count * tree_size)
    queries = rotate(
        projected[:, :query_cols].reshape(-1, kv_local * group_size, head_size), position
    ).astype(jnp.bfloat16)
    queries = queries.reshape(req_count, tree_size, kv_local, group_size, head_size).transpose(
        0, 2, 1, 3, 4
    )
    queries = queries.reshape(req_count, kv_local, query_rows, head_size)
    new_keys = rotate(
        projected[:, query_cols : query_cols + key_cols].reshape(-1, kv_local, head_size), position
    ).astype(jnp.bfloat16)
    new_keys = new_keys.reshape(req_count, tree_size, key_cols)
    new_values = (
        projected[:, query_cols + key_cols :]
        .astype(jnp.bfloat16)
        .reshape(req_count, tree_size, key_cols)
    )
    accepted_keys = jnp.take_along_axis(new_keys, accepted_index[:, :, None], axis=1)
    accepted_values = jnp.take_along_axis(new_values, accepted_index[:, :, None], axis=1)
    tree_keys = new_keys.reshape(req_count, tree_size, kv_local, head_size)
    tree_values = new_values.reshape(req_count, tree_size, kv_local, head_size)
    tree_scores = (
        jnp.einsum("rhqd,rkhd->rhqk", queries, tree_keys, preferred_element_type=jnp.float32)
        * score_scale
    )
    tree_visible = jnp.repeat(ancestry > 0.5, group_size, axis=1)[:, None]
    tree_part = absorb(
        empty_partials((req_count, kv_local, query_rows), head_size),
        tree_scores,
        tree_visible,
        lambda rounded: jnp.einsum(
            "rhqk,rkhd->rhqd", rounded, tree_values, preferred_element_type=jnp.float32
        ),
    )
    own_offsets = jnp.cumsum(own_lengths) - own_lengths
    cache_part = cache_partials(
        queries, cache_keys, cache_values, own_offsets, own_offsets + own_lengths, score_scale
    )
    local_part = combine(tree_part, cache_part)
    piece_keys = lax.all_gather(prefix_keys, "batch", axis=0, tiled=True)
    piece_values = lax.all_gather(prefix_values, "batch", axis=0, tiled=True)
    row_count = piece_keys.shape[0]
    shaped_keys = piece_keys.reshape(row_count, kv_local, head_size)
    shaped_values = piece_values.reshape(row_count, kv_local, head_size)
    slot_ids = jnp.arange(row_count, dtype=jnp.int32)
    visible = (slot_ids[None, :] < prefix_used[:, None])[:, None, None, :]
    scores = (
        jnp.einsum("rhqd,khd->rhqk", queries, shaped_keys, preferred_element_type=jnp.float32)
        * score_scale
    )
    folded = absorb(
        local_part,
        scores,
        visible,
        lambda rounded: jnp.einsum(
            "rhqk,khd->rhqd", rounded, shaped_values, preferred_element_type=jnp.float32
        ),
    )
    attended = (folded[2] / folded[1][..., None]).astype(jnp.bfloat16)
    attended = attended.reshape(req_count, kv_local, tree_size, group_size, head_size).transpose(
        0, 2, 1, 3, 4
    )
    attended = attended.reshape(req_count * tree_size, query_cols)
    mixed_rows = lax.psum_scatter(
        jnp.dot(attended, w_out, preferred_element_type=jnp.float32).astype(jnp.bfloat16),
        "tensor",
        scatter_dimension=0,
        tiled=True,
    )
    return (mixed_rows, accepted_keys, accepted_values)


def solution(mesh):
    in_specs = (
        P(("batch", "tensor"), None),
        P(),
        P(None, "tensor"),
        P(None, "tensor"),
        P(None, "tensor"),
        P("tensor", None),
        P("batch", "tensor"),
        P("batch", "tensor"),
        P("batch", "tensor"),
        P("batch", "tensor"),
        P(),
        P("batch"),
        P("batch", None),
        P("batch", None),
    )
    out_specs = (
        P(("batch", "tensor"), None),
        P("batch", None, "tensor"),
        P("batch", None, "tensor"),
    )
    return jax.shard_map(body, mesh=mesh, in_specs=in_specs, out_specs=out_specs, check_vma=False)
```

profile of v0, /device:TPU:4, one launch (start us, length us, event | category | flops | bytes accessed | tf_op | source)
XLA Modules:
  0.0 278.1 jit_solution(979624814477540230)
XLA Ops:
  8.4 1.8 fusion.54
  18.2 23.1 %all-gather.4.cloned.1.call-done = bf16[256,4096]{1,0:T(8,128)(2,1)} async-done(((bf16[32,4096]{1,0:T(8,128)(2,1)}), bf16[256,4096]{1,0:T(8,128)(2,1)}) %all-gather.4.cloned.1.call-update) | async-done | bytes 2097168 | tf_op jit(solution)/shard_map/all_gather | solution.py:144
  41.3 4.1 %fusion.85 = f32[256,512]{1,0:T(8,128)S(1)} fusion(bf16[256,4096]{1,0:T(8,128)(2,1)} %all-gather.4.cloned.1.call-done, bf16[4096,512]{1,0:T(8,128)(2,1)} %param.22), kind=kOutput, calls=%fused_computation.133 | convolution fusion | flops 1073741824 | bytes 6815744 | tf_op jit(solution)/shard_map/dot_general | solution.py:147
  46.9 44.6 %while.69 = (s32[]{:T(128)}, f32[4,1,256]{2,1,0:T(1,128)S(1)}, f32[4,1,256]{2,1,0:T(1,128)S(1)}, f32[4,1,256,128]{3,2,1,0:T(8,128)}, s32[4]{0:T(128)S(1)}, /*ind...) while((s32[]{:T(128)}, f32[4,1,256]{2,1,0:T(1,128)S(1)}, ...), condition=%wide.region_9.10_spmd, body=%wide.region_4.9_spmd.sunk | while | flops 68356632 | bytes 2712316 | solution.py:116
  50.5 4.0 %while.70 = (s32[]{:T(128)}, f32[1,256]{1,0:T(1,128)S(1)}, f32[1,256]{1,0:T(1,128)S(1)}, f32[1,256,128]{2,1,0:T(8,128)S(1)}, s32[]{:T(128)}, /*index=5*/s32[]{:T...) while((s32[]{:T(128)}, f32[1,256]{1,0:T(1,128)S(1)}, ...), condition=%wide.region_8.8_spmd, body=%wide.region_5.7_spmd.sunk | while | flops 68356616 | bytes 2181353 | solution.py:114
  53.2 1.3 fusion.119
  58.6 16.0 %while.70 = (s32[]{:T(128)}, f32[1,256]{1,0:T(1,128)S(1)}, f32[1,256]{1,0:T(1,128)S(1)}, f32[1,256,128]{2,1,0:T(8,128)S(1)}, s32[]{:T(128)}, /*index=5*/s32[]{:T...) while((s32[]{:T(128)}, f32[1,256]{1,0:T(1,128)S(1)}, ...), condition=%wide.region_8.8_spmd, body=%wide.region_5.7_spmd.sunk | while | flops 68356616 | bytes 2181353 | solution.py:114
  65.2 1.3 fusion.119
  69.2 1.3 fusion.119
  73.2 1.3 fusion.119
  78.7 4.0 %while.70 = (s32[]{:T(128)}, f32[1,256]{1,0:T(1,128)S(1)}, f32[1,256]{1,0:T(1,128)S(1)}, f32[1,256,128]{2,1,0:T(8,128)S(1)}, s32[]{:T(128)}, /*index=5*/s32[]{:T...) while((s32[]{:T(128)}, f32[1,256]{1,0:T(1,128)S(1)}, ...), condition=%wide.region_8.8_spmd, body=%wide.region_5.7_spmd.sunk | while | flops 68356616 | bytes 2181353 | solution.py:114
  81.3 1.3 fusion.119
  86.8 4.0 %while.70 = (s32[]{:T(128)}, f32[1,256]{1,0:T(1,128)S(1)}, f32[1,256]{1,0:T(1,128)S(1)}, f32[1,256,128]{2,1,0:T(8,128)S(1)}, s32[]{:T(128)}, /*index=5*/s32[]{:T...) while((s32[]{:T(128)}, f32[1,256]{1,0:T(1,128)S(1)}, ...), condition=%wide.region_8.8_spmd, body=%wide.region_5.7_spmd.sunk | while | flops 68356616 | bytes 2181353 | solution.py:114
  89.4 1.3 fusion.119
  93.3 1.5 copy.30
  94.8 1.5 copy.29
  100.0 2.6 convolution_convert_fusion.1
  102.5 22.0 %all-gather.6.cloned.1.call-done = bf16[16384,128]{1,0:T(8,128)(2,1)} async-done(((bf16[512,128]{1,0:T(8,128)(2,1)}), bf16[16384,128]{1,0:T(8,128)(2,1)}) %all-gather.6.cloned.1.call-update) | async-done | bytes 4194320 | tf_op jit(solution)/shard_map/all_gather | solution.py:196
  124.5 27.2 %fusion.17 = (f32[4,256]{1,0:T(4,128)S(1)}, f32[4,256,16384]{2,1,0:T(8,128)}) fusion(pred[4,16384]{1,0:T(4,128)(4,1)S(1)} %iota_compare_fusion, bf16[16384,128]{1,0:T(8,128)(2,1)} %all-gather.6.cloned.1.call-done, bf16[4,256,64]{2,1,0:T(8,128)(2,1)} %bitcast.194, bf16[4,256,64]{2,1,0:T(8,128)(2,1)S(1)} %bitcast.191), kind=kOutput, calls=%fused_computation.30 | convolution fusion | flops 4345822208 | bytes 71634944 | tf_op jit(solution)/shard_map/rhqd,khd->rhqk/dot_general | solution.py:204
  151.8 24.3 %fusion.18 = f32[4,256]{1,0:T(4,128)S(1)} fusion(f32[4,256,16384]{2,1,0:T(8,128)} %get-tuple-element.336, f32[4,256]{1,0:T(4,128)S(1)} %get-tuple-element.337, pred[4,16384]{1,0:T(4,128)(4,1)S(1)} %iota_compare_fusion), kind=kLoop, calls=%fused_computation.31 | loop fusion | flops 83885056 | bytes 67182592 | tf_op jit(solution)/shard_map/reduce_sum | solution.py:53
  177.3 28.4 %all-gather.8.cloned.1.call-done = bf16[16384,128]{1,0:T(8,128)(2,1)} async-done(((bf16[512,128]{1,0:T(8,128)(2,1)}), bf16[16384,128]{1,0:T(8,128)(2,1)}) %all-gather.8.cloned.1.call-update) | async-done | bytes 4194320 | tf_op jit(solution)/shard_map/all_gather | solution.py:197
  205.7 25.9 %fusion.46 = bf16[4,1,256,128]{3,2,0,1:T(8,128)(2,1)S(1)} fusion(f32[4,1,256,128]{3,2,0,1:T(8,128)S(1)} %fusion.45, bf16[16384,128]{1,0:T(8,128)(2,1)} %all-gather.8.cloned.1.call-done, f32[4,256,16384]{2,1,0:T(8,128)} %get-tuple-element.336, f32[4,256]{1,0:T(4,128)S(1)} %get-tuple-element.337, pred[4,16384]{1,0:T(4,128)(4,1)S(1)} %iota_compare_fusion, ...), kind=kOutput, calls=%fused_computation.48 | convolution fusion | flops 4379246592 | bytes 72163328 | tf_op jit(solution)/shard_map/rhqk,khd->rhqd/dot_general | solution.py:211
  231.8 4.8 %convolution_convert_fusion = bf16[256,4096]{1,0:T(8,128)(2,1)} fusion(bf16[256,512]{1,0:T(8,128)(2,1)S(1)} %reshape_transpose_reshape.4, bf16[512,4096]{1,0:T(8,128)(2,1)} %param.25), kind=kOutput, calls=%fused_computation.36 | convolution fusion | flops 1074790400 | bytes 6553600 | tf_op jit(solution)/shard_map/dot_general | solution.py:221
  238.8 32.8 %reduce-scatter.2.cloned.1.call-done = bf16[32,4096]{1,0:T(8,128)(2,1)} async-done(((bf16[256,4096]{1,0:T(8,128)(2,1)}), bf16[32,4096]{1,0:T(8,128)(2,1)}) %reduce-scatter.2.cloned.1.call-update) | async-done | bytes 262160 | tf_op jit(solution)/shard_map/reduce_scatter | solution.py:220
  (159 shorter events, 41.5 us)
Async XLA Ops:
  7.2 84.3 %copy-start = (bf16[4096,128]{1,0:T(8,128)(2,1)S(1)}, bf16[4096,128]{1,0:T(8,128)(2,1)}, u32[]{:S(2)}) copy-start(bf16[4096,128]{1,0:T(8,128)(2,1)} %param.23) | copy-start | bytes 3145732
  7.2 34.1 %all-gather.4.cloned.1.call-start = ((), (), s32[]{:S(2)}) async-start(), calls=%async_computation.1 | async-start | bytes 2359296 | tf_op jit(solution)/shard_map/all_gather | solution.py:144
  10.2 114.3 %all-gather.6.cloned.1.call-start = ((), (), s32[]{:S(2)}) async-start(), calls=%async_computation.2 | async-start | bytes 4325376 | tf_op jit(solution)/shard_map/all_gather | solution.py:196
  11.0 194.7 %all-gather.8.cloned.1.call-start = ((), (), s32[]{:S(2)}) async-start(), calls=%async_computation.3 | async-start | bytes 4325376 | tf_op jit(solution)/shard_map/all_gather | solution.py:197
  11.7 259.8 %reduce-scatter.2.cloned.1.call-start = ((), (), s32[]{:S(2)}) async-start(), calls=%async_computation.4 | async-start | bytes 2359296 | tf_op jit(solution)/shard_map/reduce_scatter | solution.py:220
  46.0 0.9 copy-start.2
  46.0 0.9 copy-start.4
  46.9 44.6 %copy-start.1 = (bf16[256,4096]{1,0:T(8,128)(2,1)S(1)}, bf16[256,4096]{1,0:T(8,128)(2,1)}, u32[]{:S(2)}) copy-start(bf16[256,4096]{1,0:T(8,128)(2,1)} %all-gather.4.cloned.1.call-done) | copy-start | bytes 6291460
  91.5 7.7 %copy-start.11 = (f32[4,1,256]{2,1,0:T(1,128)}, f32[4,1,256]{2,1,0:T(1,128)S(1)}, u32[]{:S(2)}) copy-start(f32[4,1,256]{2,1,0:T(1,128)S(1)} %get-tuple-element.269) | copy-start | bytes 12292
  91.5 33.1 %copy-start.3 = (bf16[256,4,64]{2,1,0:T(4,128)(2,1)S(1)}, bf16[256,4,64]{2,1,0:T(4,128)(2,1)}, u32[]{:S(2)}) copy-start(bf16[256,4,64]{2,1,0:T(4,128)(2,1)} %copy-done.2) | copy-start | bytes 393220
  97.2 0.6 copy-start.7
  99.2 0.7 copy-start.5
  151.8 24.4 %copy-start.12 = (f32[4,1,256]{2,1,0:T(1,128)S(1)}, f32[4,1,256]{2,1,0:T(1,128)}, u32[]{:S(2)}) copy-start(f32[4,1,256]{2,1,0:T(1,128)} %copy-done.11) | copy-start | bytes 12292
  151.8 24.5 %copy-start.6 = (f32[4,256,64]{1,2,0:T(8,128)S(1)}, f32[4,256,64]{1,2,0:T(8,128)}, u32[]{:S(2)}) copy-start(f32[4,256,64]{1,2,0:T(8,128)} %copy-done.5) | copy-start | bytes 786436
  151.8 24.4 %copy-start.9 = (bf16[256,128]{1,0:T(8,128)(2,1)S(1)}, bf16[256,128]{1,0:T(8,128)(2,1)}, u32[]{:S(2)}) copy-start(bf16[256,128]{1,0:T(8,128)(2,1)} %convolution_convert_fusion.1) | copy-start | bytes 196612
  151.8 24.4 %copy-start.10 = (f32[4,1,256,128]{3,2,1,0:T(8,128)S(1)}, f32[4,1,256,128]{3,2,1,0:T(8,128)}, u32[]{:S(2)}) copy-start(f32[4,1,256,128]{3,2,1,0:T(8,128)} %get-tuple-element.268) | copy-start | bytes 1572868
  231.8 4.9 %copy-start.13 = (s32[4,8]{1,0:T(4,128)S(1)}, s32[4,8]{1,0:T(4,128)}, u32[]{:S(2)}) copy-start(s32[4,8]{1,0:T(4,128)} %param.33) | copy-start | bytes 388
  231.8 5.6 %copy-start.8 = (bf16[4,64,128]{2,1,0:T(8,128)(2,1)S(1)}, bf16[4,64,128]{2,1,0:T(8,128)(2,1)}, u32[]{:S(2)}) copy-start(bf16[4,64,128]{2,1,0:T(8,128)(2,1)} %copy-done.7) | copy-start | bytes 196612
Sparse Core Ops, SparseCore 0:
  10.4 30.7 all-gather.3
  43.8 80.6 all-gather.5
  127.1 78.5 all-gather.7
  236.7 34.7 reduce-scatter.1
where the time goes:
time: 279 us; the launch traced here: 278 us
  waiting for transfers between devices  108 us (39%)
  matrix products  87.9 us (32%)
  other arithmetic  35.8 us (13%)
  local copies, waits for them, and re-layouts  17.8 us (6%)
  loops' own time  14.5 us (5%)
  between operations  14.2 us (5%)
    reduce_scatter x1, waiting for transfers between devices, body(): lax.psum_scatter(jnp.dot(attended, w_out, preferred_element_type=jnp.floa...  32.8 us
    all_gather x1, waiting for transfers between devices, body(): piece_values = lax.all_gather(prefix_values, 'batch', axis=0, tiled=True)  28.4 us
    dot_general x1, matrix products, body(): jnp.einsum('rhqd,khd->rhqk', queries, shaped_keys, preferred_element_type...  27.2 us
    dot_general x1, matrix products, body(): jnp.einsum('rhqk,khd->rhqd', rounded, shaped_values, preferred_element_ty...  25.9 us
    reduce_sum x9, other arithmetic, absorb(): new_sum = running_sum * factor + jnp.sum(weights, axis=-1)  25.5 us
    all_gather x1, waiting for transfers between devices, body(): piece = lax.all_gather(normed, 'tensor', axis=0, tiled=True)  23.1 us
    all_gather x1, waiting for transfers between devices, body(): piece_keys = lax.all_gather(prefix_keys, 'batch', axis=0, tiled=True)  22 us
    dot_general x7, matrix products, block_step(): jnp.einsum('hqk,khd->hqd', rounded, block_values, preferred_element_type=...  9.34 us
  transfers between devices with their start and end apart: 4, of which 4 were waited for; matrix products, arithmetic and copies ran while one was open for 38% of the time, Pallas kernels for 0%

commit v1 on v0

--- a/solution.py
+++ b/solution.py
@@ -193,7 +193,9 @@
         queries, cache_keys, cache_values, own_offsets, own_offsets + own_lengths, score_scale
     )
     local_part = combine(tree_part, cache_part)
-    piece_keys = lax.all_gather(prefix_keys, "batch", axis=0, tiled=True)
+    piece_keys = jnp.concatenate(
+        lax.all_to_all(jnp.stack([prefix_keys] * lax.axis_size("batch")), "batch", 0, 0), axis=0
+    )
     piece_values = lax.all_gather(prefix_values, "batch", axis=0, tiled=True)
     row_count = piece_keys.shape[0]
     shaped_keys = piece_keys.reshape(row_count, kv_local, head_size)

time: 279 us -> 261 us (0.935)
  waiting for transfers between devices: 108 us -> 76.9 us
  starting transfers between devices: 0.16 us -> 11.9 us
  local copies, waits for them, and re-layouts: 17.8 us -> 21.6 us
    all_to_all x0 -> x1, waiting for transfers between devices: none -> 31.5 us  [body(): lax.all_to_all(jnp.stack([prefix_keys] * lax.axis_size('batch')), 'batch'...]
    all_gather x1, waiting for transfers between devices: 28.4 us -> 0.02 us  [body(): piece_values = lax.all_gather(prefix_values, 'batch', axis=0, tiled=True)]
    all_gather x1 -> x0, waiting for transfers between devices: 22 us -> none  [body(): piece_keys = lax.all_gather(prefix_keys, 'batch', axis=0, tiled=True)]
    all_gather x1, waiting for transfers between devices: 23.1 us -> 11 us  [body(): piece = lax.all_gather(normed, 'tensor', axis=0, tiled=True)]
    all_to_all x0 -> x1, starting transfers between devices: none -> 11.8 us  [body(): lax.all_to_all(jnp.stack([prefix_keys] * lax.axis_size('batch')), 'batch'...]
    another operation x14 -> x15, local copies, waits for them, and re-layouts: 0.06 us -> 3.87 us  [the longest x1 3.81 us: body(): jnp.stack([prefix_keys] * lax.axis_size('batch'))]
  transfers between devices with their start and end apart: 4 -> 4, of which waited for: 4 -> 3; matrix products, arithmetic and copies ran while one was open for 38% -> 41% of each run, Pallas kernels for 0% -> 0%
where the time goes in v1:
time: 261 us; the launch traced here: 260 us
  matrix products  87.1 us (33%)
  waiting for transfers between devices  76.9 us (29%)
  other arithmetic  33.8 us (13%)
  local copies, waits for them, and re-layouts  21.6 us (8%)
  loops' own time  14.4 us (6%)
  between operations  14.2 us (5%)
  starting transfers between devices  11.9 us (5%)
    reduce_scatter x1, waiting for transfers between devices, body(): lax.psum_scatter(jnp.dot(attended, w_out, preferred_element_type=jnp.floa...  33.7 us
    all_to_all x1, waiting for transfers between devices, body(): lax.all_to_all(jnp.stack([prefix_keys] * lax.axis_size('batch')), 'batch'...  31.5 us
    dot_general x1, matrix products, body(): jnp.einsum('rhqd,khd->rhqk', queries, shaped_keys, preferred_element_type...  27 us
    dot_general x1, matrix products, body(): jnp.einsum('rhqk,khd->rhqd', rounded, shaped_values, preferred_element_ty...  26.1 us
    reduce_sum x9, other arithmetic, absorb(): new_sum = running_sum * factor + jnp.sum(weights, axis=-1)  25.5 us
    all_to_all x1, starting transfers between devices, body(): lax.all_to_all(jnp.stack([prefix_keys] * lax.axis_size('batch')), 'batch'...  11.8 us
    all_gather x1, waiting for transfers between devices, body(): piece = lax.all_gather(normed, 'tensor', axis=0, tiled=True)  11 us
    dot_general x7, matrix products, block_step(): jnp.einsum('hqk,khd->hqd', rounded, block_values, preferred_element_type=...  9.35 us
  transfers between devices with their start and end apart: 4, of which 3 were waited for; matrix products, arithmetic and copies ran while one was open for 41% of the time, Pallas kernels for 0%

profile of v1, /device:TPU:4, one launch (start us, length us, event | category | flops | bytes accessed | tf_op | source)
XLA Modules:
  0.0 260.0 jit_solution(16664376400438006465)
XLA Ops:
  8.4 1.8 fusion.52
  10.2 3.8 %stack.2 = bf16[32,512,128]{2,1,0:T(8,128)(2,1)} broadcast(bf16[512,128]{1,0:T(8,128)(2,1)} %param.26), dimensions={1,2} | broadcast | bytes 4325376 | tf_op jit(solution)/shard_map/stack | solution.py:197
  14.1 11.8 %all-to-all-start = ((bf16[32,512,128]{2,1,0:T(8,128)(2,1)}), bf16[32,512,128]{2,1,0:T(8,128)(2,1)}, u32[]{:S(2)}, u32[]{:S(2)}) async-start(bf16[32,512,128]{2,1,0:T(8,128)(2,1)} %stack.2), calls=%async_computation | async-start | bytes 8388608 | tf_op jit(solution)/shard_map/all_to_all | solution.py:197
  30.3 11.0 %all-gather.3.cloned.1.call-done = bf16[256,4096]{1,0:T(8,128)(2,1)} async-done(((bf16[32,4096]{1,0:T(8,128)(2,1)}), bf16[256,4096]{1,0:T(8,128)(2,1)}) %all-gather.3.cloned.1.call-update) | async-done | bytes 2097168 | tf_op jit(solution)/shard_map/all_gather | solution.py:144
  41.3 4.1 %fusion.84 = f32[256,512]{1,0:T(8,128)S(1)} fusion(bf16[256,4096]{1,0:T(8,128)(2,1)} %all-gather.3.cloned.1.call-done, bf16[4096,512]{1,0:T(8,128)(2,1)} %param.22), kind=kOutput, calls=%fused_computation.132 | convolution fusion | flops 1073741824 | bytes 6815744 | tf_op jit(solution)/shard_map/dot_general | solution.py:147
  46.9 44.5 %while.69 = (s32[]{:T(128)}, f32[4,1,256]{2,1,0:T(1,128)S(1)}, f32[4,1,256]{2,1,0:T(1,128)S(1)}, f32[4,1,256,128]{3,2,1,0:T(8,128)}, s32[4]{0:T(128)S(1)}, /*ind...) while((s32[]{:T(128)}, f32[4,1,256]{2,1,0:T(1,128)S(1)}, ...), condition=%wide.region_9.10_spmd, body=%wide.region_4.9_spmd.sunk | while | flops 68356632 | bytes 2712316 | solution.py:116
  50.5 4.0 %while.70 = (s32[]{:T(128)}, f32[1,256]{1,0:T(1,128)S(1)}, f32[1,256]{1,0:T(1,128)S(1)}, f32[1,256,128]{2,1,0:T(8,128)S(1)}, s32[]{:T(128)}, /*index=5*/s32[]{:T...) while((s32[]{:T(128)}, f32[1,256]{1,0:T(1,128)S(1)}, ...), condition=%wide.region_8.8_spmd, body=%wide.region_5.7_spmd.sunk | while | flops 68356616 | bytes 2181353 | solution.py:114
  53.2 1.3 fusion.119
  58.6 16.0 %while.70 = (s32[]{:T(128)}, f32[1,256]{1,0:T(1,128)S(1)}, f32[1,256]{1,0:T(1,128)S(1)}, f32[1,256,128]{2,1,0:T(8,128)S(1)}, s32[]{:T(128)}, /*index=5*/s32[]{:T...) while((s32[]{:T(128)}, f32[1,256]{1,0:T(1,128)S(1)}, ...), condition=%wide.region_8.8_spmd, body=%wide.region_5.7_spmd.sunk | while | flops 68356616 | bytes 2181353 | solution.py:114
  61.2 1.3 fusion.119
  65.2 1.3 fusion.119
  73.2 1.3 fusion.119
  78.6 4.0 %while.70 = (s32[]{:T(128)}, f32[1,256]{1,0:T(1,128)S(1)}, f32[1,256]{1,0:T(1,128)S(1)}, f32[1,256,128]{2,1,0:T(8,128)S(1)}, s32[]{:T(128)}, /*index=5*/s32[]{:T...) while((s32[]{:T(128)}, f32[1,256]{1,0:T(1,128)S(1)}, ...), condition=%wide.region_8.8_spmd, body=%wide.region_5.7_spmd.sunk | while | flops 68356616 | bytes 2181353 | solution.py:114
  81.3 1.3 fusion.119
  86.7 4.0 %while.70 = (s32[]{:T(128)}, f32[1,256]{1,0:T(1,128)S(1)}, f32[1,256]{1,0:T(1,128)S(1)}, f32[1,256,128]{2,1,0:T(8,128)S(1)}, s32[]{:T(128)}, /*index=5*/s32[]{:T...) while((s32[]{:T(128)}, f32[1,256]{1,0:T(1,128)S(1)}, ...), condition=%wide.region_8.8_spmd, body=%wide.region_5.7_spmd.sunk | while | flops 68356616 | bytes 2181353 | solution.py:114
  93.2 1.5 copy.30
  94.7 1.5 copy.29
  99.9 2.5 convolution_convert_fusion.1
  102.4 31.5 %all-to-all-done = bf16[32,512,128]{2,1,0:T(8,128)(2,1)} async-done(((bf16[32,512,128]{2,1,0:T(8,128)(2,1)}), bf16[32,512,128]{2,1,0:T(8,128)(2,1)}, u32[]{:S(2)}, u32[]{:S(2)}) %all-to-all-start) | async-done | bytes 4194336 | tf_op jit(solution)/shard_map/all_to_all | solution.py:197
  134.0 27.0 %fusion.17 = (f32[4,256]{1,0:T(4,128)S(1)}, f32[4,256,16384]{2,1,0:T(8,128)}) fusion(pred[4,16384]{1,0:T(4,128)(4,1)S(1)} %iota_compare_fusion, bf16[16384,128,1]{1,0,2:T(8,128)(2,1)} %bitcast.26, bf16[4,256,64]{2,1,0:T(8,128)(2,1)} %bitcast.193, bf16[4,256,64]{2,1,0:T(8,128)(2,1)S(1)} %bitcast.190), kind=kOutput, calls=%fused_computation.30 | convolution fusion | flops 4345822208 | bytes 71634944 | tf_op jit(solution)/shard_map/rhqd,khd->rhqk/dot_general | solution.py:206
  161.0 24.3 %fusion.18 = f32[4,256]{1,0:T(4,128)S(1)} fusion(f32[4,256,16384]{2,1,0:T(8,128)} %get-tuple-element.336, f32[4,256]{1,0:T(4,128)S(1)} %get-tuple-element.337, pred[4,16384]{1,0:T(4,128)(4,1)S(1)} %iota_compare_fusion), kind=kLoop, calls=%fused_computation.31 | loop fusion | flops 83885056 | bytes 67182592 | tf_op jit(solution)/shard_map/reduce_sum | solution.py:53
  186.5 26.1 %fusion.44 = bf16[4,1,256,128]{3,2,0,1:T(8,128)(2,1)S(1)} fusion(f32[4,1,256,128]{3,2,0,1:T(8,128)S(1)} %fusion.43, bf16[16384,128]{1,0:T(8,128)(2,1)} %all-gather.5.cloned.1.call-done, f32[4,256,16384]{2,1,0:T(8,128)} %get-tuple-element.336, f32[4,256]{1,0:T(4,128)S(1)} %get-tuple-element.337, pred[4,16384]{1,0:T(4,128)(4,1)S(1)} %iota_compare_fusion, ...), kind=kOutput, calls=%fused_computation.46 | convolution fusion | flops 4379246592 | bytes 72163328 | tf_op jit(solution)/shard_map/rhqk,khd->rhqd/dot_general | solution.py:213
  212.8 4.8 %convolution_convert_fusion = bf16[256,4096]{1,0:T(8,128)(2,1)} fusion(bf16[256,512]{1,0:T(8,128)(2,1)S(1)} %reshape_transpose_reshape.4, bf16[512,4096]{1,0:T(8,128)(2,1)} %param.25), kind=kOutput, calls=%fused_computation.36 | convolution fusion | flops 1074790400 | bytes 6553600 | tf_op jit(solution)/shard_map/dot_general | solution.py:223
  219.8 33.7 %reduce-scatter.2.cloned.1.call-done = bf16[32,4096]{1,0:T(8,128)(2,1)} async-done(((bf16[256,4096]{1,0:T(8,128)(2,1)}), bf16[32,4096]{1,0:T(8,128)(2,1)}) %reduce-scatter.2.cloned.1.call-update) | async-done | bytes 262160 | tf_op jit(solution)/shard_map/reduce_scatter | solution.py:222
  (165 shorter events, 39.4 us)
Async XLA Ops:
  7.2 84.3 %copy-start = (bf16[4096,128]{1,0:T(8,128)(2,1)S(1)}, bf16[4096,128]{1,0:T(8,128)(2,1)}, u32[]{:S(2)}) copy-start(bf16[4096,128]{1,0:T(8,128)(2,1)} %param.23) | copy-start | bytes 3145732
  7.2 34.1 %all-gather.3.cloned.1.call-start = ((), (), s32[]{:S(2)}) async-start(), calls=%async_computation.2 | async-start | bytes 2359296 | tf_op jit(solution)/shard_map/all_gather | solution.py:144
  14.0 12.6 %copy-start.14 = (s32[4]{0:T(128)S(1)}, s32[4]{0:T(128)}, u32[]{:S(2)}) copy-start(s32[4]{0:T(128)} %param.31) | copy-start | bytes 52
  14.0 12.8 %copy-start.15 = (s32[128]{0:T(128)S(1)}, s32[128]{0:T(128)}, u32[]{:S(2)}) copy-start(s32[128]{0:T(128)} %param.30) | copy-start | bytes 1540
  14.0 13.1 %copy-start.16 = (s32[4,64]{1,0:T(4,128)S(1)}, s32[4,64]{1,0:T(4,128)}, u32[]{:S(2)}) copy-start(s32[4,64]{1,0:T(4,128)} %param.32) | copy-start | bytes 3076
  14.1 119.9 %all-to-all-start = ((bf16[32,512,128]{2,1,0:T(8,128)(2,1)}), bf16[32,512,128]{2,1,0:T(8,128)(2,1)}, u32[]{:S(2)}, u32[]{:S(2)}) async-start(bf16[32,512,128]{2,1,0:T(8,128)(2,1)} %stack.2), calls=%async_computation | async-start | bytes 8388608 | tf_op jit(solution)/shard_map/all_to_all | solution.py:197
  25.8 160.7 %all-gather.5.cloned.1.call-start = ((), (), s32[]{:S(2)}) async-start(), calls=%async_computation.3 | async-start | bytes 4325376 | tf_op jit(solution)/shard_map/all_gather | solution.py:199
  26.6 226.9 %reduce-scatter.2.cloned.1.call-start = ((), (), s32[]{:S(2)}) async-start(), calls=%async_computation.4 | async-start | bytes 2359296 | tf_op jit(solution)/shard_map/reduce_scatter | solution.py:222
  46.0 0.9 copy-start.2
  46.0 0.9 copy-start.4
  46.9 44.5 %copy-start.1 = (bf16[256,4096]{1,0:T(8,128)(2,1)S(1)}, bf16[256,4096]{1,0:T(8,128)(2,1)}, u32[]{:S(2)}) copy-start(bf16[256,4096]{1,0:T(8,128)(2,1)} %all-gather.3.cloned.1.call-done) | copy-start | bytes 6291460
  91.4 7.7 %copy-start.11 = (f32[4,1,256]{2,1,0:T(1,128)}, f32[4,1,256]{2,1,0:T(1,128)S(1)}, u32[]{:S(2)}) copy-start(f32[4,1,256]{2,1,0:T(1,128)S(1)} %get-tuple-element.269) | copy-start | bytes 12292
  91.4 42.5 %copy-start.3 = (bf16[256,4,64]{2,1,0:T(4,128)(2,1)S(1)}, bf16[256,4,64]{2,1,0:T(4,128)(2,1)}, u32[]{:S(2)}) copy-start(bf16[256,4,64]{2,1,0:T(4,128)(2,1)} %copy-done.2) | copy-start | bytes 393220
  97.1 0.6 copy-start.7
  99.1 0.7 copy-start.5
  161.0 24.4 %copy-start.12 = (f32[4,1,256]{2,1,0:T(1,128)S(1)}, f32[4,1,256]{2,1,0:T(1,128)}, u32[]{:S(2)}) copy-start(f32[4,1,256]{2,1,0:T(1,128)} %copy-done.11) | copy-start | bytes 12292
  161.0 24.5 %copy-start.6 = (f32[4,256,64]{1,2,0:T(8,128)S(1)}, f32[4,256,64]{1,2,0:T(8,128)}, u32[]{:S(2)}) copy-start(f32[4,256,64]{1,2,0:T(8,128)} %copy-done.5) | copy-start | bytes 786436
  161.0 24.4 %copy-start.9 = (bf16[256,128]{1,0:T(8,128)(2,1)S(1)}, bf16[256,128]{1,0:T(8,128)(2,1)}, u32[]{:S(2)}) copy-start(bf16[256,128]{1,0:T(8,128)(2,1)} %convolution_convert_fusion.1) | copy-start | bytes 196612
  161.0 24.4 %copy-start.10 = (f32[4,1,256,128]{3,2,1,0:T(8,128)S(1)}, f32[4,1,256,128]{3,2,1,0:T(8,128)}, u32[]{:S(2)}) copy-start(f32[4,1,256,128]{3,2,1,0:T(8,128)} %get-tuple-element.268) | copy-start | bytes 1572868
  212.8 4.9 %copy-start.13 = (s32[4,8]{1,0:T(4,128)S(1)}, s32[4,8]{1,0:T(4,128)}, u32[]{:S(2)}) copy-start(s32[4,8]{1,0:T(4,128)} %param.33) | copy-start | bytes 388
  212.8 5.7 %copy-start.8 = (bf16[4,64,128]{2,1,0:T(8,128)(2,1)S(1)}, bf16[4,64,128]{2,1,0:T(8,128)(2,1)}, u32[]{:S(2)}) copy-start(bf16[4,64,128]{2,1,0:T(8,128)(2,1)} %copy-done.7) | copy-start | bytes 196612
Sparse Core Ops, SparseCore 0:
  10.4 30.7 all-gather.2
  43.8 103.3 all-gather.4
  217.8 35.6 reduce-scatter.1
